TPU v7x, 32 devices: a whole 2x2x4 slice. The times are simulated.
32 devices in a mesh: groups: 2 (over x), seq: 16 (over z, y, core).
Axes of the slice: x: 2, y: 2, z: 4, core: 2. Of those that a mesh axis runs over, the one named last changes fastest.
Arguments:
- hidden_in: bfloat16 [32768, 2048], P(('groups', 'seq')), parts along dimension 0, may hold values from -6 to 6
- queries: bfloat16 [32768, 1024], P(('groups', 'seq')), parts along dimension 0, may hold values from -6 to 6
- kv_weight: bfloat16 [2048, 2048], replicated, may hold values from -0.125 to 0.125
- level_weight: float32 [16, 8], replicated, may hold values from 0.3 to 3
Outputs:
- attended: bfloat16 [32768, 1024], P(('groups', 'seq')), parts along dimension 0
There are 2 independent parts, one for each index of `groups`. A program takes and returns all parts, laid end to end along the dimension named above; an argument that names none is the same for every part. Nothing has to cross between parts.
All inputs are finite; a program needn't handle non-finite values.
Results may differ from a plain program's by a relative error of at most 0.0034.
Values sent between devices are 32-bit elements; how exact they have to be, the bound alone decides.
No kernel may reach another device: no remote copies, remote signals or barrier semaphores. Data moves between devices by JAX's collectives and lax.ppermute only.
A program may use at most 128 MiB of HBM per device.

v0:
```python
import jax
import jax.numpy as jnp
from jax import lax
from jax.sharding import PartitionSpec as P

HEADS = 8
HEAD = 128
SPAN = 64


def swapped(x, axis, distance):
    return lax.ppermute(x, axis, [(i, i ^ 1 << distance) for i in range(lax.axis_size(axis))])


def in_span(query_blocks, keys, values, level_weight):
    causal = jnp.tril(jnp.ones((SPAN, SPAN), jnp.float32))
    diag_scale = level_weight[0] / jnp.sqrt(jnp.float32(SPAN * HEAD))
    scores = jnp.einsum("jtha,jsha->jhts", query_blocks, keys, preferred_element_type=jnp.float32)
    scores = (scores * diag_scale[None, :, None, None] * causal[None, None]).astype(jnp.bfloat16)
    return jnp.einsum("jhts,jshb->jthb", scores, values, preferred_element_type=jnp.float32)


def remote_states(total, level_weight, local_bits, tokens):
    index = lax.axis_index("seq")
    depth = lax.axis_size("seq").bit_length() - 1
    remote = jnp.zeros_like(total)
    block = total
    for level in range(depth):
        bit = jnp.right_shift(index, level) & 1
        partner = swapped(block, "seq", level)
        factor = level_weight[1 + local_bits + level] / jnp.sqrt(jnp.float32(2**level * tokens))
        remote = remote + bit.astype(jnp.float32) * factor[:, None, None] * partner
        block = block + partner
    return remote


def local(hidden_in, queries, kv_weight, level_weight):
    tokens = hidden_in.shape[0]
    width = HEADS * HEAD
    count = tokens // SPAN
    local_bits = count.bit_length() - 1
    highest = lax.Precision.HIGHEST
    kv = jnp.dot(hidden_in, kv_weight, preferred_element_type=jnp.float32).astype(jnp.bfloat16)
    keys = kv[:, :width].reshape(count, SPAN, HEADS, HEAD)
    values = kv[:, width:].reshape(count, SPAN, HEADS, HEAD)
    query_blocks = queries.reshape(count, SPAN, HEADS, HEAD)
    span_states = jnp.einsum("jcha,jchb->jhab", keys, values, preferred_element_type=jnp.float32)
    total = jnp.sum(span_states, axis=0)
    remote = remote_states(total, level_weight, local_bits, tokens)
    intra = in_span(query_blocks, keys, values, level_weight)
    target = jnp.arange(count, dtype=jnp.int32)[:, None]
    source = jnp.arange(count, dtype=jnp.int32)[None, :]
    coef = jnp.zeros((count, count, HEADS), jnp.float32)
    for level in range(local_bits):
        member = jnp.right_shift(target, level) & 1 == 1
        member = member & (jnp.right_shift(source, level + 1) == jnp.right_shift(target, level + 1))
        member = member & (jnp.right_shift(source, level) & 1 == 0)
        factor = level_weight[1 + level] / jnp.sqrt(jnp.float32(2**level * SPAN))
        coef = coef + member.astype(jnp.float32)[:, :, None] * factor[None, None, :]
    local_states = jnp.einsum("jih,ihab->jhab", coef, span_states, precision=highest)
    states = local_states + remote[None]
    inter = jnp.einsum(
        "jtha,jhab->jthb", query_blocks.astype(jnp.float32), states, precision=highest
    )
    inter = inter / jnp.sqrt(jnp.float32(HEAD))
    return (intra + inter).astype(jnp.bfloat16).reshape(tokens, width)


def solution(mesh):
    in_specs = (P(("groups", "seq"), None), P(("groups", "seq"), None), P(), P())
    out_specs = P(("groups", "seq"), None)
    return jax.shard_map(local, mesh=mesh, in_specs=in_specs, out_specs=out_specs, check_vma=False)
```

profile of v0, /device:TPU:0, one launch (start us, length us, event | category | flops | bytes accessed | tf_op | source)
XLA Modules:
  0.0 98.0 jit_solution(12695792420870214556)
XLA Ops:
  0.0 12.5 %convolution_convert_fusion = bf16[1024,2048]{1,0:T(8,128)(2,1)S(1)} fusion(bf16[1024,2048]{1,0:T(8,128)(2,1)} %param.4, bf16[2048,2048]{1,0:T(8,128)(2,1)} %param.6), kind=kOutput, calls=%fused_computation.9 | convolution fusion | flops 8592031744 | bytes 16777216 | tf_op jit(solution)/shard_map/dot_general | solution.py:43
  12.5 1.2 %slice_bitcast_fusion.1 = (bf16[128,8,8,128]{3,1,2,0:T(8,128)(2,1)S(1)}, bf16[128,8,8,128]{3,1,2,0:T(8,128)(2,1)S(1)}) fusion(bf16[1024,2048]{1,0:T(8,128)(2,1)S(1)} %convolution_convert_fusion), kind=kLoop, calls=%fused_computation.13 | loop fusion | bytes 8388608
  13.7 0.6 copy.19
  14.3 0.6 copy.17
  14.9 0.0 copy-start
  14.9 0.0 copy-start.2
  15.0 4.7 %fusion.24 = (f32[8,128,128]{2,1,0:T(8,128)S(1)}, f32[16,8,128,128]{3,2,1,0:T(8,128)}) fusion(bf16[16,64,8,128]{3,2,1,0:T(8,128)(2,1)S(1)} %bitcast.34, bf16[16,64,8,128]{3,2,1,0:T(8,128)(2,1)S(1)} %bitcast.36), kind=kOutput, calls=%fused_computation.52 | convolution fusion | flops 270401536 | bytes 13107200 | tf_op jit(solution)/shard_map/jcha,jchb->jhab/dot_general | solution.py:47
  19.6 0.5 collective-permute-start
  20.2 0.1 and_convert_fusion
  20.3 0.3 multiply_reduce_fusion.3
  20.6 0.1 and_convert_fusion.1
  20.7 0.1 and_convert_fusion.2
  20.8 1.0 %collective-permute-done = f32[8,128,128]{2,1,0:T(8,128)} collective-permute-done((f32[8,128,128]{2,1,0:T(8,128)S(1)}, f32[8,128,128]{2,1,0:T(8,128)}, u32[]{:S(2)}, u32[]{:S(2)}) %collective-permute-start) | collective-permute-done | bytes 524320 | tf_op jit(solution)/shard_map/ppermute | solution.py:12
  21.8 1.1 %add.45 = f32[8,128,128]{2,1,0:T(8,128)S(1)} add(f32[8,128,128]{2,1,0:T(8,128)S(1)} %get-tuple-element.16, f32[8,128,128]{2,1,0:T(8,128)} %collective-permute-done) | non-fusion elementwise | flops 131072 | bytes 1572864 | tf_op jit(solution)/shard_map/add | solution.py:33
  22.9 2.9 %collective-permute-start.1 = (f32[8,128,128]{2,1,0:T(8,128)S(1)}, f32[8,128,128]{2,1,0:T(8,128)S(1)}, u32[]{:S(2)}, u32[]{:S(2)}) collective-permute-start(f32[8,128,128]{2,1,0:T(8,128)S(1)} %add.45), channel_id=1, source_target_pairs={{0,2},{1,3},{2,0},{3,1},{4,6},{5,7},{6,4},{7,5},{8,10},{9,11},{10,... | collective-permute-start | bytes 1572872 | tf_op jit(solution)/shard_map/ppermute | solution.py:12
  25.8 0.1 and_convert_fusion.3
  25.9 0.2 add_bitcast_fusion
  26.1 0.1 copy.15
  26.2 3.5 %copy.18 = bf16[128,8,8,128]{3,2,1,0:T(8,128)(2,1)} copy(bf16[128,8,8,128]{3,1,2,0:T(8,128)(2,1)} %bitcast.41) | data formatting | bytes 4194304
  29.8 8.3 %collective-permute-done.1 = f32[8,128,128]{2,1,0:T(8,128)S(1)} collective-permute-done((f32[8,128,128]{2,1,0:T(8,128)S(1)}, f32[8,128,128]{2,1,0:T(8,128)S(1)}, u32[]{:S(2)}, u32[]{:S(2)}) %collective-permute-start.1) | collective-permute-done | bytes 524320 | tf_op jit(solution)/shard_map/ppermute | solution.py:12
  38.0 0.1 add.47
  38.1 1.9 %collective-permute-start.2 = (f32[8,128,128]{2,1,0:T(8,128)S(1)}, f32[8,128,128]{2,1,0:T(8,128)S(1)}, u32[]{:S(2)}, u32[]{:S(2)}) collective-permute-start(f32[8,128,128]{2,1,0:T(8,128)S(1)} %add.47), channel_id=1, source_target_pairs={{0,4},{1,5},{2,6},{3,7},{4,0},{5,1},{6,2},{7,3},{8,12},{9,13},{10,... | collective-permute-start | bytes 1572872 | tf_op jit(solution)/shard_map/ppermute | solution.py:12
  40.0 17.0 %fusion.2 = f32[8,128,128,16]{2,3,1,0:T(8,128)} fusion(f32[16,16,8,1]{0,1,3,2:T(8,128)S(1)} %copy.15, f32[16,8,128,128]{3,2,1,0:T(8,128)} %get-tuple-element.17), kind=kOutput, calls=%fused_computation.3 | convolution fusion | flops 402653184 | bytes 16785408 | tf_op jit(solution)/shard_map/jih,ihab->jhab/dot_general | solution.py:60
  57.0 0.0 collective-permute-done.2
  57.0 0.9 add.49
  57.9 2.6 %collective-permute-start.3 = (f32[8,128,128]{2,1,0:T(8,128)}, f32[8,128,128]{2,1,0:T(8,128)}, u32[]{:S(2)}, u32[]{:S(2)}) collective-permute-start(f32[8,128,128]{2,1,0:T(8,128)} %add.49), channel_id=1, source_target_pairs={{0,8},{1,9},{2,10},{3,11},{4,12},{5,13},{6,14},{7,15},{8,0},{9,1},... | collective-permute-start | bytes 1572872 | tf_op jit(solution)/shard_map/ppermute | solution.py:12
  60.5 6.0 %fusion.15 = f32[16,8,128,64]{2,3,1,0:T(8,128)} fusion(bf16[16,64,8,128]{3,2,1,0:T(8,128)(2,1)S(1)} %bitcast.35, f32[64,64]{1,0:T(8,128)S(1)} %fusion.21, f32[8]{0:T(128)S(1)} %get-tuple-element.11, bf16[16,64,8,128]{3,2,1,0:T(8,128)(2,1)} %bitcast.38, bf16[16,64,8,128]{3,2,1,0:T(8,128)(2,1)} %bitcast.37), kind=kOutput, calls=%fused_computation.20 | convolution fusion | flops 270008320 | bytes 10502176 | tf_op jit(solution)/shard_map/jhts,jshb->jthb/dot_general | solution.py:20
  66.5 16.6 %collective-permute-done.3 = f32[8,128,128]{2,1,0:T(8,128)} collective-permute-done((f32[8,128,128]{2,1,0:T(8,128)}, f32[8,128,128]{2,1,0:T(8,128)}, u32[]{:S(2)}, u32[]{:S(2)}) %collective-permute-start.3) | collective-permute-done | bytes 524320 | tf_op jit(solution)/shard_map/ppermute | solution.py:12
  83.1 1.4 %multiply_add_fusion = f32[8,128,128]{2,1,0:T(8,128)S(1)} fusion(f32[8,128,128]{2,1,0:T(8,128)} %collective-permute-done.3, f32[8,128,128]{2,1,0:T(8,128)S(1)} %collective-permute-done.2, f32[8,128,128]{2,1,0:T(8,128)S(1)} %collective-permute-done.1, f32[8,128,128]{2,1,0:T(8,128)} %collective-permute-done, f32[8]{0:T(128)S(1)} %get-tuple-element.12, ...), kind=kLoop, calls=%fused_computation.22 | loop fusion | flops 917504 | bytes 2621568 | tf_op jit(solution)/shard_map/add | solution.py:32
  84.6 9.7 %fusion.6 = bf16[16,64,8,128]{3,1,2,0:T(8,128)(2,1)S(1)} fusion(f32[16,8,128,64]{2,3,1,0:T(8,128)} %fusion.15, f32[8,128,128,16]{2,3,1,0:T(8,128)} %fusion.2, f32[8,128,128]{2,1,0:T(8,128)S(1)} %multiply_add_fusion, bf16[16,64,8,128]{3,2,1,0:T(8,128)(2,1)S(1)} %bitcast.39), kind=kOutput, calls=%fused_computation.10 | convolution fusion | flops 1615855616 | bytes 17301504 | tf_op jit(solution)/shard_map/jtha,jhab->jthb/dot_general | solution.py:62
  94.3 1.8 %copy.13 = bf16[16,64,8,128]{3,2,1,0:T(8,128)(2,1)S(1)} copy(bf16[16,64,8,128]{3,1,2,0:T(8,128)(2,1)S(1)} %fusion.6) | data formatting | bytes 4194304 | tf_op jit(solution)/shard_map/convert_element_type | solution.py:66
  96.1 2.0 %copy.50 = bf16[128,8,8,128]{3,1,2,0:T(8,128)(2,1)} copy(bf16[128,8,8,128]{3,2,1,0:T(8,128)(2,1)S(1)} %bitcast.40) | data formatting | bytes 4194304
  (13 shorter events, 0.1 us)
Async XLA Ops:
  14.9 4.7 %copy-start = (bf16[128,8,8,128]{3,2,1,0:T(8,128)(2,1)}, bf16[128,8,8,128]{3,2,1,0:T(8,128)(2,1)S(1)}, u32[]{:S(2)}) copy-start(bf16[128,8,8,128]{3,2,1,0:T(8,128)(2,1)S(1)} %copy.17) | copy-start | bytes 6291460
  14.9 5.3 %copy-start.2 = (f32[16,8]{0,1:T(8,128)S(1)}, f32[16,8]{0,1:T(8,128)}, u32[]{:S(2)}) copy-start(f32[16,8]{0,1:T(8,128)} %param.7) | copy-start | bytes 1540
  19.6 2.2 %collective-permute-start = (f32[8,128,128]{2,1,0:T(8,128)S(1)}, f32[8,128,128]{2,1,0:T(8,128)}, u32[]{:S(2)}, u32[]{:S(2)}) collective-permute-start(f32[8,128,128]{2,1,0:T(8,128)S(1)} %get-tuple-element.16), channel_id=1, source_target_pairs={{0,1},{1,0},{2,3},{3,2},{4,5},{5,4},{6,7},{7,6},{8,9},{9,8},{10,11... | collective-permute-start | bytes 1572872 | tf_op jit(solution)/shard_map/ppermute | solution.py:12
  22.9 15.2 %collective-permute-start.1 = (f32[8,128,128]{2,1,0:T(8,128)S(1)}, f32[8,128,128]{2,1,0:T(8,128)S(1)}, u32[]{:S(2)}, u32[]{:S(2)}) collective-permute-start(f32[8,128,128]{2,1,0:T(8,128)S(1)} %add.45), channel_id=1, source_target_pairs={{0,2},{1,3},{2,0},{3,1},{4,6},{5,7},{6,4},{7,5},{8,10},{9,11},{10,... | collective-permute-start | bytes 1572872 | tf_op jit(solution)/shard_map/ppermute | solution.py:12
  38.1 18.9 %collective-permute-start.2 = (f32[8,128,128]{2,1,0:T(8,128)S(1)}, f32[8,128,128]{2,1,0:T(8,128)S(1)}, u32[]{:S(2)}, u32[]{:S(2)}) collective-permute-start(f32[8,128,128]{2,1,0:T(8,128)S(1)} %add.47), channel_id=1, source_target_pairs={{0,4},{1,5},{2,6},{3,7},{4,0},{5,1},{6,2},{7,3},{8,12},{9,13},{10,... | collective-permute-start | bytes 1572872 | tf_op jit(solution)/shard_map/ppermute | solution.py:12
  57.9 25.2 %collective-permute-start.3 = (f32[8,128,128]{2,1,0:T(8,128)}, f32[8,128,128]{2,1,0:T(8,128)}, u32[]{:S(2)}, u32[]{:S(2)}) collective-permute-start(f32[8,128,128]{2,1,0:T(8,128)} %add.49), channel_id=1, source_target_pairs={{0,8},{1,9},{2,10},{3,11},{4,12},{5,13},{6,14},{7,15},{8,0},{9,1},... | collective-permute-start | bytes 1572872 | tf_op jit(solution)/shard_map/ppermute | solution.py:12
  66.5 18.1 %copy-start.1 = (bf16[128,8,8,128]{3,2,1,0:T(8,128)(2,1)S(1)}, bf16[128,8,8,128]{3,2,1,0:T(8,128)(2,1)}, u32[]{:S(2)}) copy-start(bf16[128,8,8,128]{3,2,1,0:T(8,128)(2,1)} %copy.18) | copy-start | bytes 6291460
where the time goes:
time: 98.2 us; the launch traced here: 98 us
  matrix products  49.8 us (51%)
  waiting for transfers between devices  25.9 us (26%)
  local copies, waits for them, and re-layouts  9.83 us (10%)
  starting transfers between devices  7.88 us (8%)
  other arithmetic  4.38 us (4%)
    ppermute x4, waiting for transfers between devices, swapped(): lax.ppermute(x, axis, [(i, i ^ 1 << distance) for i in range(lax.axis_siz...  25.9 us
    dot_general x1, matrix products, local(): jnp.einsum('jih,ihab->jhab', coef, span_states, precision=highest)  17 us
    dot_general x1, matrix products, local(): jnp.dot(hidden_in, kv_weight, preferred_element_type=jnp.float32)  12.5 us
    dot_general x1, matrix products, local(): jnp.einsum('jtha,jhab->jthb', query_blocks.astype(jnp.float32), states, p...  9.69 us
    unnamed x11, local copies, waits for them, and re-layouts  7.94 us
    ppermute x4, starting transfers between devices, swapped(): lax.ppermute(x, axis, [(i, i ^ 1 << distance) for i in range(lax.axis_siz...  7.88 us
    dot_general x1, matrix products, in_span(): jnp.einsum('jhts,jshb->jthb', scores, values, preferred_element_type=jnp....  6 us
    dot_general x1, matrix products, local(): jnp.einsum('jcha,jchb->jhab', keys, values, preferred_element_type=jnp.fl...  4.66 us
  transfers between devices with their start and end apart: 4, of which 3 were waited for; matrix products, arithmetic and copies ran while one was open for 28% of the time, Pallas kernels for 0%

commit v1 on v0

v1 whole, which is shorter than its diff:
```python
import functools
import math

import jax
import jax.numpy as jnp
from jax import lax
from jax.experimental import pallas as pl
from jax.experimental.pallas import tpu as pltpu
from jax.sharding import PartitionSpec as P


HEAD = 128
SPAN = 64
CHUNK = 256
PAIR = 2 * HEAD
MIB = 1 << 20

BF16 = jnp.bfloat16
F32 = jnp.float32
VMEM = pl.BlockSpec(memory_space=pltpu.VMEM)
HBM = pl.BlockSpec(memory_space=pltpu.MemorySpace.HBM)
SMEM = pl.BlockSpec(memory_space=pltpu.SMEM)


def in_hbm(x):
    return pltpu.with_memory_space_constraint(x, pltpu.MemorySpace.HBM)


def own_pair():
    index = lax.axis_index("seq")
    return (index & 1) * 2 + (index >> 1 & 1)


def dot(a, b):
    return jnp.dot(a, b, preferred_element_type=F32)


def outer(a, b):
    return lax.dot_general(a, b, (((0,), (0,)), ((), ())), preferred_element_type=F32)


def pair_states(k_ref, v_ref, column, s_ref, first):
    for i in range(2):
        at = slice(column + i * HEAD, column + (i + 1) * HEAD)
        s_ref[first + i] = outer(k_ref[:, at], v_ref[:, at])


def first_kernel(h_hbm, w_hbm, k_ref, v_ref, s_ref, h_ref, w_rest, w_first, h_sem, w_sem):
    tokens, width = h_hbm.shape[0], w_hbm.shape[1] // 2
    rows = tokens // 4
    own = own_pair()

    def load_w(n):
        pair, part = n // 2, n % 2
        column = pl.multiple_of((own ^ (3 - pair)) * PAIR + part * width, PAIR)
        target = w_first.at[n] if n < 4 else w_rest.at[n - 4]
        return pltpu.make_async_copy(w_hbm.at[:, pl.ds(column, PAIR)], target, w_sem.at[n])

    def load_h(r):
        at = pl.ds(r * rows, rows)
        return pltpu.make_async_copy(h_hbm.at[at, :], h_ref.at[at, :], h_sem.at[r])

    weights = [load_w(n) for n in range(8)]
    hidden = [load_h(r) for r in range(4)]
    for copy in [weights[0], hidden[0], weights[1]] + hidden[1:] + weights[2:]:
        copy.start()
    weights[0].wait()
    for r in range(4):
        at = slice(r * rows, (r + 1) * rows)
        hidden[r].wait()
        k_ref[at, :PAIR] = dot(h_ref[at, :], w_first[0]).astype(BF16)
        if r == 0:
            weights[1].wait()
        v_ref[at, :PAIR] = dot(h_ref[at, :], w_first[1]).astype(BF16)
    weights[2].wait()
    k_ref[:, PAIR:] = dot(h_ref[...], w_first[2]).astype(BF16)
    weights[3].wait()
    v_ref[:, PAIR:] = dot(h_ref[...], w_first[3]).astype(BF16)
    pair_states(k_ref, v_ref, 0, s_ref, 0)
    pair_states(k_ref, v_ref, PAIR, s_ref, 2)
    for n in range(4, 8):
        weights[n].wait()


def next_kernel(pair, h_ref, w_rest, k_ref, v_ref, s_ref):
    k_ref[...] = dot(h_ref[...], w_rest[2 * pair]).astype(BF16)
    v_ref[...] = dot(h_ref[...], w_rest[2 * pair + 1]).astype(BF16)
    pair_states(k_ref, v_ref, 0, s_ref, 0)


def project(hidden_in, kv_weight):
    tokens, depth = hidden_in.shape
    bf = lambda *shape: jax.ShapeDtypeStruct(shape, BF16)
    state = lambda n: jax.ShapeDtypeStruct((n, HEAD, HEAD), F32)
    flops = 2 * tokens * depth * PAIR
    k0, v0, s0, hidden, w_rest = pl.pallas_call(
        first_kernel,
        in_specs=[HBM, HBM],
        out_specs=[VMEM] * 5,
        out_shape=[bf(tokens, 2 * PAIR), bf(tokens, 2 * PAIR), state(4), bf(tokens, depth), bf(4, depth, PAIR)],
        scratch_shapes=[
            pltpu.VMEM((4, depth, PAIR), BF16),
            pltpu.SemaphoreType.DMA((4,)),
            pltpu.SemaphoreType.DMA((8,)),
        ],
        cost_estimate=pl.CostEstimate(flops=4 * flops, bytes_accessed=12 * MIB, transcendentals=0),
        compiler_params=pltpu.CompilerParams(vmem_limit_bytes=20 * MIB),
        name="kv_first",
    )(in_hbm(hidden_in), in_hbm(kv_weight))
    parts = [(k0, v0, s0)]
    for pair in range(2):
        parts.append(
            pl.pallas_call(
                functools.partial(next_kernel, pair),
                in_specs=[VMEM, VMEM],
                out_specs=[VMEM] * 3,
                out_shape=[bf(tokens, PAIR), bf(tokens, PAIR), state(2)],
                cost_estimate=pl.CostEstimate(flops=2 * flops, bytes_accessed=8 * MIB, transcendentals=0),
                compiler_params=pltpu.CompilerParams(vmem_limit_bytes=4 * MIB),
                name="kv_next",
            )(hidden, w_rest)
        )
    return parts


def split_state(state):
    high = state.astype(BF16)
    low = (state - high.astype(F32)).astype(BF16)
    return jnp.concatenate([high, low], axis=0)


def local_kernel(first, own_ref, lw_ref, q_ref, k_ref, v_ref, o_ref, mask_ref):
    head = pl.program_id(0)
    tokens = q_ref.shape[0]
    chunks = tokens // CHUNK
    actual = (own_ref[0] ^ (3 - (first + head) // 2)) * 2 + head % 2
    scale = lambda level: lw_ref[actual, 1 + level] * F32(1.0 / math.sqrt(2**level * SPAN * HEAD))
    diagonal = lw_ref[actual, 0] * F32(1.0 / math.sqrt(SPAN * HEAD))
    row = lax.broadcasted_iota(jnp.int32, (CHUNK, CHUNK), 0)
    col = lax.broadcasted_iota(jnp.int32, (CHUNK, CHUNK), 1)
    apart = (row // SPAN) ^ (col // SPAN)
    mask = jnp.where(apart == 0, diagonal, jnp.where(apart == 1, scale(0), scale(1)))
    mask_ref[...] = jnp.where(row >= col, mask, 0.0)
    lanes = pl.ds(pl.multiple_of(head * HEAD, HEAD), HEAD)
    rows = [pl.ds(c * CHUNK, CHUNK) for c in range(chunks)]
    sums = {}
    for c in range(chunks - 1):
        sums[(0, c)] = outer(k_ref[rows[c], lanes], v_ref[rows[c], lanes])
    levels = chunks.bit_length() - 1
    for level in range(levels - 1):
        for b in range((chunks >> (level + 1)) - 1):
            sums[(level + 1, b)] = sums[(level, 2 * b)] + sums[(level, 2 * b + 1)]
    for c in range(chunks):
        q = q_ref[rows[c], :]
        k = k_ref[rows[c], lanes]
        v = v_ref[rows[c], lanes]
        scores = lax.dot_general(q, k, (((1,), (1,)), ((), ())), preferred_element_type=F32)
        scores = (scores * mask_ref[...]).astype(BF16)
        result = dot(scores, v)
        if c:
            state = None
            for level in range(levels):
                if (c >> level) & 1:
                    term = scale(level + 2) * sums[(level, (c >> level) - 1)]
                    state = term if state is None else state + term
            result = result + dot(jnp.concatenate([q, q], axis=1), split_state(state))
        o_ref[rows[c], :] = result


def local_part(own, level_weight, queries, keys, values, first):
    tokens = queries.shape[0]
    heads = keys.shape[1] // HEAD
    spec = pltpu.PrefetchScalarGridSpec(
        num_scalar_prefetch=1,
        grid=(heads,),
        in_specs=[
            SMEM,
            pl.BlockSpec((tokens, HEAD), lambda j, own: (0, (own[0] ^ (3 - (first + j) // 2)) * 2 + j % 2)),
            VMEM,
            VMEM,
        ],
        out_specs=pl.BlockSpec((tokens, HEAD), lambda j, own: (0, j)),
        scratch_shapes=[pltpu.VMEM((CHUNK, CHUNK), F32)],
    )
    return pl.pallas_call(
        functools.partial(local_kernel, first),
        grid_spec=spec,
        out_shape=jax.ShapeDtypeStruct((tokens, heads * HEAD), F32),
        cost_estimate=pl.CostEstimate(flops=heads * 200 * 10**6, bytes_accessed=heads * MIB, transcendentals=0),
        compiler_params=pltpu.CompilerParams(vmem_limit_bytes=12 * MIB),
        name="local_part",
    )(own, level_weight, queries, keys, values)


def factors(lw_ref, level, tokens, pair):
    own = own_pair()
    head = (own ^ (3 - pair)) * 2
    at = 1 + (tokens // SPAN).bit_length() - 1 + level
    scale = F32(1.0 / math.sqrt(2**level * tokens * HEAD))
    return [lw_ref[head + i, at] * scale for i in range(2)]


def taken(level):
    return (lax.axis_index("seq") >> level & 1).astype(F32)


def add_kernel(a_ref, b_ref, o_ref):
    o_ref[...] = a_ref[...] + b_ref[...]


def widen_kernel(tokens, lw_ref, s_ref, half_ref, quarter_ref, *refs):
    gots, (send_ref, far_ref) = refs[:-2], refs[-2:]
    near = factors(lw_ref, 1, tokens, 3)
    levels = [factors(lw_ref, 2 + n, tokens, 3) for n in range(len(gots))]
    for i in range(2):
        far = sum((taken(2 + n) * levels[n][i]) * gots[n][i] for n in range(len(gots)))
        send_ref[i] = far + ((1.0 - taken(1)) * near[i]) * (s_ref[i] + half_ref[2 + i])
        far_ref[i] = far + (taken(1) * near[i]) * quarter_ref[i]


def share_kernel(tokens, lw_ref, s2_ref, s3_ref, far2_ref, far3_ref, send_ref):
    for pair, far_ref, s_ref in ((2, far2_ref, s2_ref), (3, far3_ref, s3_ref)):
        near = factors(lw_ref, 0, tokens, pair)
        for i in range(2):
            send_ref[2 * pair - 4 + i] = far_ref[i] + ((1.0 - taken(0)) * near[i]) * s_ref[i]


def small(kernel, heads, count, specs, *operands):
    return pl.pallas_call(
        kernel,
        in_specs=specs,
        out_specs=[VMEM] * count,
        out_shape=[jax.ShapeDtypeStruct((heads, HEAD, HEAD), F32)] * count,
        cost_estimate=pl.CostEstimate(flops=10**6, bytes_accessed=MIB // 2, transcendentals=0),
        compiler_params=pltpu.CompilerParams(vmem_limit_bytes=2 * MIB),
    )(*operands)


def final_kernel(first, own_ref, lw_ref, q_ref, a_ref, r_ref, *rest):
    o_ref = rest[-1]
    head = pl.program_id(0)
    tokens = q_ref.shape[0]
    q = q_ref[...]
    state = r_ref[0]
    if first >= 4:
        near = factors(lw_ref, 0, tokens, first // 2)
        weight = taken(0) * jnp.where(head == 0, near[0], near[1])
        state = state + weight * rest[0][0]
    far = dot(jnp.concatenate([q, q], axis=1), split_state(state))
    o_ref[...] = (a_ref[...] + far).astype(BF16)


def final_part(own, level_weight, queries, local, remote, first, half=None, previous=None):
    tokens, width = queries.shape
    heads = local.shape[1] // HEAD
    place = lambda j, own: (0, (own[0] ^ (3 - (first + j) // 2)) * 2 + j % 2)
    in_specs = [
        SMEM,
        pl.BlockSpec((tokens, HEAD), place),
        pl.BlockSpec((tokens, HEAD), lambda j, own: (0, j)),
        pl.BlockSpec((1, HEAD, HEAD), lambda j, own: (j, 0, 0)),
    ]
    operands = [level_weight, queries, local, remote]
    if half is not None:
        in_specs.append(pl.BlockSpec((1, HEAD, HEAD), lambda j, own: (first - 4 + j, 0, 0)))
        operands.append(half)
    aliases = {}
    if previous is not None:
        in_specs.append(HBM)
        operands.append(previous)
        aliases = {len(operands): 0}
    return pl.pallas_call(
        functools.partial(final_kernel, first),
        grid_spec=pltpu.PrefetchScalarGridSpec(
            num_scalar_prefetch=1,
            grid=(heads,),
            in_specs=in_specs,
            out_specs=pl.BlockSpec((tokens, HEAD), place),
        ),
        out_shape=jax.ShapeDtypeStruct((tokens, width), BF16),
        input_output_aliases=aliases,
        cost_estimate=pl.CostEstimate(flops=heads * 70 * 10**6, bytes_accessed=heads * MIB, transcendentals=0),
        compiler_params=pltpu.CompilerParams(vmem_limit_bytes=12 * MIB),
        name="final_part",
    )(own, *operands)


def exchange(x, level):
    size = lax.axis_size("seq")
    return lax.ppermute(x, "seq", [(i, i ^ 1 << level) for i in range(size)])


def upward(x, level):
    size = lax.axis_size("seq")
    return lax.ppermute(x, "seq", [(i, i + (1 << level)) for i in range(size) if not i >> level & 1])


def layer(hidden_in, queries, kv_weight, level_weight):
    tokens = hidden_in.shape[0]
    depth = lax.axis_size("seq").bit_length() - 1
    own = own_pair().reshape(1)
    weights = level_weight.T

    (k0, v0, s0), (k2, v2, s2), (k3, v3, s3) = project(hidden_in, kv_weight)
    half = exchange(s0, 0)
    quarter = exchange(s2 + half[:2], 1)
    block = s3 + half[2:] + quarter

    local0 = local_part(own, weights, queries, k0, v0, 0)
    local2 = local_part(own, weights, queries, k2, v2, 4)
    local3 = local_part(own, weights, queries, k3, v3, 6)

    gots = []
    for level in range(2, depth - 1):
        gots.append(exchange(block, level))
        (block,) = small(add_kernel, 2, 1, [VMEM] * 2, block, gots[-1])
    gots.append(upward(block, depth - 1))
    send, far3 = small(
        functools.partial(widen_kernel, tokens), 2, 2,
        [SMEM] + [VMEM] * (3 + len(gots)), weights, s3, half, quarter, *gots,
    )
    far2 = exchange(send, 1)
    (send,) = small(
        functools.partial(share_kernel, tokens), 4, 1,
        [SMEM] + [VMEM] * 4, weights, s2, s3, far2, far3,
    )
    far01 = exchange(send, 0)

    out = final_part(own, weights, queries, local3, far3, 6, half)
    out = final_part(own, weights, queries, local2, far2, 4, half, out)
    return final_part(own, weights, queries, local0, far01, 0, None, out)


def solution(mesh):
    in_specs = (P(("groups", "seq"), None), P(("groups", "seq"), None), P(), P())
    out_specs = P(("groups", "seq"), None)
    return jax.shard_map(layer, mesh=mesh, in_specs=in_specs, out_specs=out_specs, check_vma=False)
```

time: 98.2 us -> 62.3 us (0.63)
  the two profiles are of different devices: /device:TPU:0 before, /device:TPU:25 now
where the time goes in v1:
time: 62.3 us; the launch traced here: 61.9 us
  Pallas kernels  35.7 us (57%)
  waiting for transfers between devices  15.5 us (25%)
  starting transfers between devices  7.48 us (12%)
  local copies, waits for them, and re-layouts  2.93 us (5%)
    pallas_call x1, Pallas kernels, project(): pl.pallas_call(first_kernel, in_specs=[HBM, HBM], out_specs=[VMEM] * 5, o...  11.1 us
    pallas_call x3, Pallas kernels, local_part(): pl.pallas_call(functools.partial(local_kernel, first), grid_spec=spec, ou...  8.95 us
    ppermute x1, waiting for transfers between devices, upward(): lax.ppermute(x, 'seq', [(i, i + (1 << level)) for i in range(size) if not...  8.64 us
    pallas_call x3, Pallas kernels, final_part(): pl.pallas_call(functools.partial(final_kernel, first), grid_spec=pltpu.Pr...  8.26 us
    ppermute x5, waiting for transfers between devices, exchange(): return lax.ppermute(x, 'seq', [(i, i ^ 1 << level) for i in range(size)])  6.87 us
    ppermute x5, starting transfers between devices, exchange(): return lax.ppermute(x, 'seq', [(i, i ^ 1 << level) for i in range(size)])  6.01 us
    pallas_call x2, Pallas kernels, project(): pl.pallas_call(functools.partial(next_kernel, pair), in_specs=[VMEM, VMEM...  5.38 us
    unnamed x28, local copies, waits for them, and re-layouts  2.93 us
  transfers between devices with their start and end apart: 6, of which 4 were waited for; matrix products, arithmetic and copies ran while one was open for 0% of the time, Pallas kernels for 30%

profile of v1, /device:TPU:25, one launch (start us, length us, event | category | flops | bytes accessed | tf_op | source)
XLA Modules:
  0.0 61.9 jit_solution(16974532440637553419)
XLA Ops:
  0.0 11.1 %kv_first.1 = (bf16[1024,512]{1,0:T(8,128)(2,1)S(1)}, bf16[1024,512]{1,0:T(8,128)(2,1)S(1)}, f32[4,128,128]{2,1,0:T(8,128)S(1)}, bf16[1024,2048]{1,0:T(8,128)(2,1)S(1)}, bf16[4,2048,256]{2,1,0:T(8,128)(2,1)S(1)}) custom-call(bf16[1024,2048]{1,0:T(8,128)(2,1)} %h_hbm.1, bf16[2048,2048]{1,0:T(8,128)(2,1)} %w_hbm.1), custom_call_target="tpu_custom_call" | custom-call | flops 4294967296 | bytes 12582912 | tf_op jit(solution)/shard_map/kv_first/pallas_call | solution.py:96
  11.1 0.0 copy-start.1
  11.1 0.7 %collective-permute-start = (f32[4,128,128]{2,1,0:T(8,128)S(1)}, f32[4,128,128]{2,1,0:T(8,128)S(1)}, u32[]{:S(2)}, u32[]{:S(2)}) collective-permute-start(f32[4,128,128]{2,1,0:T(8,128)S(1)} %get-tuple-element.24), channel_id=1, source_target_pairs={{0,1},{1,0},{2,3},{3,2},{4,5},{5,4},{6,7},{7,6},{8,9},{9,8},{10,11... | collective-permute-start | bytes 786440 | tf_op jit(solution)/shard_map/ppermute | solution.py:290
  11.9 2.7 %kv_next.2 = (bf16[1024,256]{1,0:T(8,128)(2,1)S(1)}, bf16[1024,256]{1,0:T(8,128)(2,1)S(1)}, f32[2,128,128]{2,1,0:T(8,128)S(1)}) custom-call(bf16[1024,2048]{1,0:T(8,128)(2,1)S(1)} %get-tuple-element.20.h_ref, bf16[4,2048,256]{2,1,0:T(8,128)(2,1)S(1)} %get-tuple-element.21.w_rest), custom_call_target="tpu_custom_call" | custom-call | flops 2147483648 | bytes 8388608 | tf_op jit(solution)/shard_map/kv_next/pallas_call | solution.py:113
  14.6 0.0 copy-done.1
  14.6 0.0 copy-start.3
  14.6 0.0 copy-start.5
  14.6 0.0 collective-permute-done.half_ref.rest_0_
  14.6 0.0 copy-start.13
  14.6 1.3 %collective-permute-start.1 = (f32[2,128,128]{2,1,0:T(8,128)S(1)}, f32[2,128,128]{2,1,0:T(8,128)S(1)}, u32[]{:S(2)}, u32[]{:S(2)}) collective-permute-start(f32[2,128,128]{2,1,0:T(8,128)S(1)} %slice_add_fusion.1), channel_id=1, source_target_pairs={{0,2},{1,3},{2,0},{3,1},{4,6},{5,7},{6,4},{7,5},{8,10},{9,11},{10,... | collective-permute-start | bytes 393224 | tf_op jit(solution)/shard_map/ppermute | solution.py:290
  15.9 2.7 %kv_next.3 = (bf16[1024,256]{1,0:T(8,128)(2,1)S(1)}, bf16[1024,256]{1,0:T(8,128)(2,1)S(1)}, f32[2,128,128]{2,1,0:T(8,128)S(1)}) custom-call(bf16[1024,2048]{1,0:T(8,128)(2,1)S(1)} %get-tuple-element.20.h_ref, bf16[4,2048,256]{2,1,0:T(8,128)(2,1)S(1)} %get-tuple-element.21.w_rest), custom_call_target="tpu_custom_call" | custom-call | flops 2147483648 | bytes 8388608 | tf_op jit(solution)/shard_map/kv_next/pallas_call | solution.py:113
  18.7 0.8 %copy-done.9 = bf16[1024,256]{1,0:T(8,128)(2,1)} copy-done((bf16[1024,256]{1,0:T(8,128)(2,1)}, bf16[1024,256]{1,0:T(8,128)(2,1)S(1)}, u32[]{:S(2)}) %copy-start.9) | copy-done | bytes 524312
  19.5 0.3 collective-permute-done.1.quarter_ref
  19.8 0.2 collective-permute-start.2
  20.0 4.0 %collective-permute-done.2.b_ref.refs_0_ = f32[2,128,128]{2,1,0:T(8,128)S(1)} collective-permute-done((f32[2,128,128]{2,1,0:T(8,128)S(1)}, f32[2,128,128]{2,1,0:T(8,128)S(1)}, u32[]{:S(2)}, u32[]{:S(2)}) %collective-permute-start.2) | collective-permute-done | bytes 131104 | tf_op jit(solution)/shard_map/ppermute | solution.py:290
  24.0 1.5 %collective-permute-start.3 = (f32[2,128,128]{2,1,0:T(8,128)S(1)}, f32[2,128,128]{2,1,0:T(8,128)S(1)}, u32[]{:S(2)}, u32[]{:S(2)}) collective-permute-start(f32[2,128,128]{2,1,0:T(8,128)S(1)} %shard_map.46), channel_id=1, source_target_pairs={{0,8},{1,9},{2,10},{3,11},{4,12},{5,13},{6,14},{7,15},{16,24},{17,... | collective-permute-start | bytes 393224 | tf_op jit(solution)/shard_map/ppermute | solution.py:295
  25.5 8.6 %collective-permute-done.3.refs_1_ = f32[2,128,128]{2,1,0:T(8,128)S(1)} collective-permute-done((f32[2,128,128]{2,1,0:T(8,128)S(1)}, f32[2,128,128]{2,1,0:T(8,128)S(1)}, u32[]{:S(2)}, u32[]{:S(2)}) %collective-permute-start.3) | collective-permute-done | bytes 131104 | tf_op jit(solution)/shard_map/ppermute | solution.py:295
  34.2 0.7 %shard_map.47 = (f32[2,128,128]{2,1,0:T(8,128)S(1)}, f32[2,128,128]{2,1,0:T(8,128)S(1)}) custom-call(f32[8,16]{1,0:T(8,128)S(1)} %bitcast.2, f32[2,128,128]{2,1,0:T(8,128)S(1)} %get-tuple-element.23.s_ref.s3_ref, f32[4,128,128]{2,1,0:T(8,128)S(1)} %collective-permute-done.half_ref.rest_0_, f32[2,128,128]{2,1,0:T(8,128)S(1)} %collective-permute-done.1.quarter_ref, ...), custom_call_target="tpu_custom_call" | custom-call | flops 1000000 | bytes 524288 | tf_op jit(solution)/shard_map/pallas_call | solution.py:229
  34.8 1.3 %collective-permute-start.4 = (f32[2,128,128]{2,1,0:T(8,128)S(1)}, f32[2,128,128]{2,1,0:T(8,128)S(1)}, u32[]{:S(2)}, u32[]{:S(2)}) collective-permute-start(f32[2,128,128]{2,1,0:T(8,128)S(1)} %get-tuple-element.25), channel_id=1, source_target_pairs={{0,2},{1,3},{2,0},{3,1},{4,6},{5,7},{6,4},{7,5},{8,10},{9,11},{10,... | collective-permute-start | bytes 393224 | tf_op jit(solution)/shard_map/ppermute | solution.py:290
  36.2 2.6 %collective-permute-done.4.far2_ref.r_ref = f32[2,128,128]{2,1,0:T(8,128)S(1)} collective-permute-done((f32[2,128,128]{2,1,0:T(8,128)S(1)}, f32[2,128,128]{2,1,0:T(8,128)S(1)}, u32[]{:S(2)}, u32[]{:S(2)}) %collective-permute-start.4) | collective-permute-done | bytes 131104 | tf_op jit(solution)/shard_map/ppermute | solution.py:290
  38.7 1.3 %shard_map.48 = f32[4,128,128]{2,1,0:T(8,128)} custom-call(f32[8,16]{1,0:T(8,128)S(1)} %bitcast.3, f32[2,128,128]{2,1,0:T(8,128)S(1)} %get-tuple-element.22.s2_ref, f32[2,128,128]{2,1,0:T(8,128)S(1)} %get-tuple-element.23.s_ref.s3_ref, f32[2,128,128]{2,1,0:T(8,128)S(1)} %collective-permute-done.4.far2_ref.r_ref, ...), custom_call_target="tpu_custom_call" | custom-call | flops 1000000 | bytes 524288 | tf_op jit(solution)/shard_map/pallas_call | solution.py:229
  40.1 2.4 %collective-permute-start.5 = (f32[4,128,128]{2,1,0:T(8,128)}, f32[4,128,128]{2,1,0:T(8,128)}, u32[]{:S(2)}, u32[]{:S(2)}) collective-permute-start(f32[4,128,128]{2,1,0:T(8,128)} %shard_map.48), channel_id=1, source_target_pairs={{0,1},{1,0},{2,3},{3,2},{4,5},{5,4},{6,7},{7,6},{8,9},{9,8},{10,11... | collective-permute-start | bytes 786440 | tf_op jit(solution)/shard_map/ppermute | solution.py:290
  42.5 1.0 %copy-done.4 = bf16[1024,256]{1,0:T(8,128)(2,1)S(1)} copy-done((bf16[1024,256]{1,0:T(8,128)(2,1)S(1)}, bf16[1024,256]{1,0:T(8,128)(2,1)}, u32[]{:S(2)}) %copy-start.4) | copy-done | bytes 524312
  43.6 1.0 %copy-done.6 = bf16[1024,256]{1,0:T(8,128)(2,1)S(1)} copy-done((bf16[1024,256]{1,0:T(8,128)(2,1)S(1)}, bf16[1024,256]{1,0:T(8,128)(2,1)}, u32[]{:S(2)}) %copy-start.6) | copy-done | bytes 524312
  44.6 2.3 %local_part.4.a_ref = f32[1024,256]{1,0:T(8,128)S(1)} custom-call(s32[1]{0:T(128)} %bitcast.own_ref, f32[8,16]{1,0:T(8,128)S(1)} %bitcast.4, bf16[1024,1024]{1,0:T(8,128)(2,1)S(1)} %copy-done, bf16[1024,256]{1,0:T(8,128)(2,1)S(1)} %copy-done.4, bf16[1024,256]{1,0:T(8,128)(2,1)S(1)} %copy-done.6), custom_call_target="tpu_custom_call" | custom-call | flops 400000000 | bytes 2097152 | tf_op jit(solution)/shard_map/local_part/pallas_call | solution.py:185
  47.0 0.0 copy-start.2
  47.0 2.4 %local_part.5.a_ref = f32[1024,256]{1,0:T(8,128)S(1)} custom-call(s32[1]{0:T(128)} %bitcast.own_ref, f32[8,16]{1,0:T(8,128)S(1)} %bitcast.5, bf16[1024,1024]{1,0:T(8,128)(2,1)S(1)} %copy-done, bf16[1024,256]{1,0:T(8,128)(2,1)S(1)} %copy-done.8, bf16[1024,256]{1,0:T(8,128)(2,1)S(1)} %copy-done.10), custom_call_target="tpu_custom_call" | custom-call | flops 400000000 | bytes 2097152 | tf_op jit(solution)/shard_map/local_part/pallas_call | solution.py:185
  49.4 4.2 %local_part.3.a_ref = f32[1024,512]{1,0:T(8,128)S(1)} custom-call(s32[1]{0:T(128)} %bitcast.own_ref, f32[8,16]{1,0:T(8,128)S(1)} %bitcast.6, bf16[1024,1024]{1,0:T(8,128)(2,1)S(1)} %copy-done, bf16[1024,512]{1,0:T(8,128)(2,1)S(1)} %get-tuple-element.18.k_ref, bf16[1024,512]{1,0:T(8,128)(2,1)S(1)} %copy-done.2), custom_call_target="tpu_custom_call" | custom-call | flops 800000000 | bytes 4194304 | tf_op jit(solution)/shard_map/local_part/pallas_call | solution.py:185
  53.6 2.2 %final_part.3.rest_1_ = bf16[1024,1024]{1,0:T(8,128)(2,1)} custom-call(s32[1]{0:T(128)} %bitcast.own_ref, f32[8,16]{1,0:T(8,128)S(1)} %bitcast.7, bf16[1024,1024]{1,0:T(8,128)(2,1)S(1)} %copy-done, f32[1024,256]{1,0:T(8,128)S(1)} %local_part.5.a_ref, f32[2,128,128]{2,1,0:T(8,128)S(1)} %copy-done.12, f32[4,128,128]{2,1,0:T(8,128)S(1)} %collective-permute-done.half_ref.rest_0_), custom_call_target="tpu_custom_call" | custom-call | flops 140000000 | bytes 2097152 | tf_op jit(solution)/shard_map/final_part/pallas_call | solution.py:272
  55.8 2.1 %final_part.4.rest_0_ = bf16[1024,1024]{1,0:T(8,128)(2,1)} custom-call(s32[1]{0:T(128)} %bitcast.own_ref, f32[8,16]{1,0:T(8,128)S(1)} %bitcast.8, bf16[1024,1024]{1,0:T(8,128)(2,1)S(1)} %copy-done, f32[1024,256]{1,0:T(8,128)S(1)} %local_part.4.a_ref, f32[2,128,128]{2,1,0:T(8,128)S(1)} %collective-permute-done.4.far2_ref.r_ref, ...), custom_call_target="tpu_custom_call", output_to_operand_aliasing={{}: (6, {})} | custom-call | flops 140000000 | bytes 2097152 | tf_op jit(solution)/shard_map/final_part/pallas_call | solution.py:272
  57.9 0.0 collective-permute-done.5.r_ref
  57.9 4.0 %final_part.5 = bf16[1024,1024]{1,0:T(8,128)(2,1)} custom-call(s32[1]{0:T(128)} %bitcast.own_ref, f32[8,16]{1,0:T(8,128)S(1)} %bitcast.9, bf16[1024,1024]{1,0:T(8,128)(2,1)S(1)} %copy-done, f32[1024,512]{1,0:T(8,128)S(1)} %local_part.3.a_ref, f32[4,128,128]{2,1,0:T(8,128)} %collective-permute-done.5.r_ref, ...), custom_call_target="tpu_custom_call", output_to_operand_aliasing={{}: (5, {})} | custom-call | flops 280000000 | bytes 4194304 | tf_op jit(solution)/shard_map/final_part/pallas_call | solution.py:272
  (22 shorter events, 0.1 us)
Async XLA Ops:
  11.1 3.4 %copy-start.1 = (bf16[1024,512]{1,0:T(8,128)(2,1)}, bf16[1024,512]{1,0:T(8,128)(2,1)S(1)}, u32[]{:S(2)}) copy-start(bf16[1024,512]{1,0:T(8,128)(2,1)S(1)} %get-tuple-element.19.v_ref) | copy-start | bytes 3145732
  11.1 3.5 %collective-permute-start = (f32[4,128,128]{2,1,0:T(8,128)S(1)}, f32[4,128,128]{2,1,0:T(8,128)S(1)}, u32[]{:S(2)}, u32[]{:S(2)}) collective-permute-start(f32[4,128,128]{2,1,0:T(8,128)S(1)} %get-tuple-element.24), channel_id=1, source_target_pairs={{0,1},{1,0},{2,3},{3,2},{4,5},{5,4},{6,7},{7,6},{8,9},{9,8},{10,11... | collective-permute-start | bytes 786440 | tf_op jit(solution)/shard_map/ppermute | solution.py:290
  14.6 4.1 %copy-start.3 = (bf16[1024,256]{1,0:T(8,128)(2,1)}, bf16[1024,256]{1,0:T(8,128)(2,1)S(1)}, u32[]{:S(2)}) copy-start(bf16[1024,256]{1,0:T(8,128)(2,1)S(1)} %get-tuple-element.27.k_ref) | copy-start | bytes 1572868
  14.6 4.1 %copy-start.5 = (bf16[1024,256]{1,0:T(8,128)(2,1)}, bf16[1024,256]{1,0:T(8,128)(2,1)S(1)}, u32[]{:S(2)}) copy-start(bf16[1024,256]{1,0:T(8,128)(2,1)S(1)} %get-tuple-element.28.v_ref) | copy-start | bytes 1572868
  14.6 19.5 %copy-start.13 = (f32[16,8]{0,1:T(8,128)S(1)}, f32[16,8]{0,1:T(8,128)}, u32[]{:S(2)}) copy-start(f32[16,8]{0,1:T(8,128)} %param.7) | copy-start | bytes 1540
  14.6 5.1 %collective-permute-start.1 = (f32[2,128,128]{2,1,0:T(8,128)S(1)}, f32[2,128,128]{2,1,0:T(8,128)S(1)}, u32[]{:S(2)}, u32[]{:S(2)}) collective-permute-start(f32[2,128,128]{2,1,0:T(8,128)S(1)} %slice_add_fusion.1), channel_id=1, source_target_pairs={{0,2},{1,3},{2,0},{3,1},{4,6},{5,7},{6,4},{7,5},{8,10},{9,11},{10,... | collective-permute-start | bytes 393224 | tf_op jit(solution)/shard_map/ppermute | solution.py:290
  18.7 0.8 %copy-start.9 = (bf16[1024,256]{1,0:T(8,128)(2,1)}, bf16[1024,256]{1,0:T(8,128)(2,1)S(1)}, u32[]{:S(2)}) copy-start(bf16[1024,256]{1,0:T(8,128)(2,1)S(1)} %get-tuple-element.30.v_ref) | copy-start | bytes 1572868
  19.5 20.6 %copy-start.7 = (bf16[1024,256]{1,0:T(8,128)(2,1)}, bf16[1024,256]{1,0:T(8,128)(2,1)S(1)}, u32[]{:S(2)}) copy-start(bf16[1024,256]{1,0:T(8,128)(2,1)S(1)} %get-tuple-element.29.k_ref) | copy-start | bytes 1572868
  19.5 23.0 %copy-start = (bf16[1024,1024]{1,0:T(8,128)(2,1)S(1)}, bf16[1024,1024]{1,0:T(8,128)(2,1)}, u32[]{:S(2)}) copy-start(bf16[1024,1024]{1,0:T(8,128)(2,1)} %q_ref.11) | copy-start | bytes 6291460
  19.8 4.2 %collective-permute-start.2 = (f32[2,128,128]{2,1,0:T(8,128)S(1)}, f32[2,128,128]{2,1,0:T(8,128)S(1)}, u32[]{:S(2)}, u32[]{:S(2)}) collective-permute-start(f32[2,128,128]{2,1,0:T(8,128)S(1)} %fusion.a_ref), channel_id=1, source_target_pairs={{0,4},{1,5},{2,6},{3,7},{4,0},{5,1},{6,2},{7,3},{8,12},{9,13},{10,... | collective-permute-start | bytes 393224 | tf_op jit(solution)/shard_map/ppermute | solution.py:290
  24.0 10.1 %collective-permute-start.3 = (f32[2,128,128]{2,1,0:T(8,128)S(1)}, f32[2,128,128]{2,1,0:T(8,128)S(1)}, u32[]{:S(2)}, u32[]{:S(2)}) collective-permute-start(f32[2,128,128]{2,1,0:T(8,128)S(1)} %shard_map.46), channel_id=1, source_target_pairs={{0,8},{1,9},{2,10},{3,11},{4,12},{5,13},{6,14},{7,15},{16,24},{17,... | collective-permute-start | bytes 393224 | tf_op jit(solution)/shard_map/ppermute | solution.py:295
  34.8 7.7 %copy-start.11 = (f32[2,128,128]{2,1,0:T(8,128)}, f32[2,128,128]{2,1,0:T(8,128)S(1)}, u32[]{:S(2)}) copy-start(f32[2,128,128]{2,1,0:T(8,128)S(1)} %get-tuple-element.26.far3_ref.r_ref) | copy-start | bytes 393220
  34.8 3.9 %collective-permute-start.4 = (f32[2,128,128]{2,1,0:T(8,128)S(1)}, f32[2,128,128]{2,1,0:T(8,128)S(1)}, u32[]{:S(2)}, u32[]{:S(2)}) collective-permute-start(f32[2,128,128]{2,1,0:T(8,128)S(1)} %get-tuple-element.25), channel_id=1, source_target_pairs={{0,2},{1,3},{2,0},{3,1},{4,6},{5,7},{6,4},{7,5},{8,10},{9,11},{10,... | collective-permute-start | bytes 393224 | tf_op jit(solution)/shard_map/ppermute | solution.py:290
  40.1 17.8 %collective-permute-start.5 = (f32[4,128,128]{2,1,0:T(8,128)}, f32[4,128,128]{2,1,0:T(8,128)}, u32[]{:S(2)}, u32[]{:S(2)}) collective-permute-start(f32[4,128,128]{2,1,0:T(8,128)} %shard_map.48), channel_id=1, source_target_pairs={{0,1},{1,0},{2,3},{3,2},{4,5},{5,4},{6,7},{7,6},{8,9},{9,8},{10,11... | collective-permute-start | bytes 786440 | tf_op jit(solution)/shard_map/ppermute | solution.py:290
  42.5 1.0 %copy-start.4 = (bf16[1024,256]{1,0:T(8,128)(2,1)S(1)}, bf16[1024,256]{1,0:T(8,128)(2,1)}, u32[]{:S(2)}) copy-start(bf16[1024,256]{1,0:T(8,128)(2,1)} %copy-done.3) | copy-start | bytes 1572868
  43.6 1.0 %copy-start.6 = (bf16[1024,256]{1,0:T(8,128)(2,1)S(1)}, bf16[1024,256]{1,0:T(8,128)(2,1)}, u32[]{:S(2)}) copy-start(bf16[1024,256]{1,0:T(8,128)(2,1)} %copy-done.5) | copy-start | bytes 1572868
  44.6 2.3 %copy-start.8 = (bf16[1024,256]{1,0:T(8,128)(2,1)S(1)}, bf16[1024,256]{1,0:T(8,128)(2,1)}, u32[]{:S(2)}) copy-start(bf16[1024,256]{1,0:T(8,128)(2,1)} %copy-done.7) | copy-start | bytes 1572868
  44.6 2.4 %copy-start.10 = (bf16[1024,256]{1,0:T(8,128)(2,1)S(1)}, bf16[1024,256]{1,0:T(8,128)(2,1)}, u32[]{:S(2)}) copy-start(bf16[1024,256]{1,0:T(8,128)(2,1)} %copy-done.9) | copy-start | bytes 1572868
  47.0 2.4 %copy-start.2 = (bf16[1024,512]{1,0:T(8,128)(2,1)S(1)}, bf16[1024,512]{1,0:T(8,128)(2,1)}, u32[]{:S(2)}) copy-start(bf16[1024,512]{1,0:T(8,128)(2,1)} %copy-done.1) | copy-start | bytes 3145732
  49.4 4.3 %copy-start.12 = (f32[2,128,128]{2,1,0:T(8,128)S(1)}, f32[2,128,128]{2,1,0:T(8,128)}, u32[]{:S(2)}) copy-start(f32[2,128,128]{2,1,0:T(8,128)} %copy-done.11) | copy-start | bytes 393220
